TPU v7x, 32 devices: a whole 2x2x4 slice. The times are simulated.
32 devices in a mesh: clips: 2 (over y), space: 4 (over z), tm: 2 (over x), chan: 2 (over core).
Axes of the slice: x: 2, y: 2, z: 4, core: 2. Of those that a mesh axis runs over, the one named last changes fastest.
Arguments:
- frames_in: bfloat16 [4, 16, 160, 384], P(('clips', 'tm'), 'space', None, 'chan'), parts along dimension 0, may hold values from -6 to 6
- cache: bfloat16 [4, 16, 160, 384], P('clips', 'space'), parts along dimension 0, may hold values from -6 to 6
- gain_one: bfloat16 [384], replicated, may hold values from 0.099609375 to 1.8984375
- gain_two: bfloat16 [384], replicated, may hold values from 0.099609375 to 1.8984375
- w_query: bfloat16 [384, 384], replicated, may hold values from -10 to 10
- w_key: bfloat16 [384, 384], replicated, may hold values from -10 to 10
- w_value: bfloat16 [384, 384], replicated, may hold values from -0.3125 to 0.3125
- w_out: bfloat16 [384, 384], replicated, may hold values from -0.3125 to 0.3125
- conv_weight: bfloat16 [3, 3, 3, 384, 384], P(None, None, None, None, 'chan'), may hold values from -0.0625 to 0.0625
Outputs:
- decoded: bfloat16 [4, 16, 160, 384], P(('clips', 'tm'), 'space', None, 'chan'), parts along dimension 0
There are 2 independent parts, one for each index of `clips`. A program takes and returns all parts, laid end to end along the dimension named above; an argument that names none is the same for every part. Nothing has to cross between parts.
All inputs are finite; a program needn't handle non-finite values.
Results may differ from a plain program's by a relative error of at most 0.0062.
Values may be sent and summed in bfloat16 or wider, within the bound.
A program may use at most 128 MiB of HBM per device.

v0:
```python
import jax
import jax.numpy as jnp
from jax import lax
from jax.sharding import PartitionSpec as P


def from_behind(array, axis, by):
    devices = lax.axis_size(axis)
    pairs = [(i, i + by) for i in range(devices) if 0 <= i + by < devices]
    return lax.ppermute(array, axis, pairs)


def padded_2(cells, sides, width):
    for axis, dim in sides:
        count = lax.axis_size(axis)
        ends = count - 1
        head = lax.slice_in_dim(cells, 0, width, axis=dim)
        tail = lax.slice_in_dim(cells, cells.shape[dim] - width, cells.shape[dim], axis=dim)
        cells = jnp.concatenate(
            [
                lax.ppermute(tail, axis, [(i, (i + 1) % count) for i in range(ends)]),
                cells,
                lax.ppermute(head, axis, [((i + 1) % count, i) for i in range(ends)]),
            ],
            axis=dim,
        )
    return cells


def rms_scaled(values, gain):
    wide = values.astype(jnp.float32)
    factor = lax.rsqrt(jnp.mean(wide * wide, axis=-1, keepdims=True) + 1e-06)
    return wide * factor * gain.astype(jnp.float32)


def body(frames_in, cache, gain_one, gain_two, w_query, w_key, w_value, w_out, conv_weight):
    mine = lax.axis_index("chan")
    own = lax.all_to_all(frames_in, "chan", split_axis=1, concat_axis=3, tiled=True)
    half_rows, cells, width = (own.shape[1], own.shape[2], own.shape[3])
    tokens = own.reshape(half_rows * cells, width)
    normed = rms_scaled(tokens, gain_one).astype(jnp.bfloat16)
    query = jnp.dot(normed, w_query, preferred_element_type=jnp.float32).astype(jnp.bfloat16)
    scale = width ** (-0.5)
    count = tokens.shape[0]
    piece = lax.all_gather(normed, ("space", "chan"), axis=0, tiled=True)
    keys = jnp.dot(piece, w_key, preferred_element_type=jnp.float32).astype(jnp.bfloat16)
    values = jnp.dot(piece, w_value, preferred_element_type=jnp.float32).astype(jnp.bfloat16)
    top = jnp.full((count, 1), -1e30, jnp.float32)
    scores = jnp.einsum("qc,kc->qk", query, keys, preferred_element_type=jnp.float32) * scale
    new_top = jnp.maximum(top, jnp.max(scores, axis=-1, keepdims=True))
    weights = jnp.exp(scores - new_top)
    total = jnp.sum(weights, axis=-1, keepdims=True)
    accum = jnp.dot(weights.astype(jnp.bfloat16), values, preferred_element_type=jnp.float32)
    top, total, accum = (new_top, total, accum)
    attended = (accum / total).astype(jnp.bfloat16)
    joined = tokens.astype(jnp.float32) + jnp.dot(
        attended, w_out, preferred_element_type=jnp.float32
    )
    joined = joined.astype(jnp.bfloat16).reshape(1, half_rows, cells, width)
    whole = lax.all_gather(joined, "chan", axis=1, tiled=True)
    act = jax.nn.silu(rms_scaled(whole, gain_two)).astype(jnp.bfloat16)
    moment = lax.axis_index("tm")
    first = from_behind(act, "tm", 1)
    second = from_behind(act, "tm", 2)
    prev_one = jnp.where(moment == 0, cache[1:2], first)
    prev_two = jnp.where(moment == 0, cache[0:1], jnp.where(moment == 1, cache[1:2], second))
    stacked = jnp.concatenate([prev_two, prev_one, act], axis=0)
    rimmed = padded_2(stacked, (("space", 1),), 1)
    padded = jnp.pad(rimmed, ((0, 0), (0, 0), (1, 1), (0, 0)))
    conv = lax.conv_general_dilated(
        padded[None],
        conv_weight,
        (1, 1, 1),
        "VALID",
        dimension_numbers=("NDHWC", "DHWIO", "NDHWC"),
        preferred_element_type=jnp.float32,
    )[0]
    share = conv_weight.shape[4]
    own_joined = lax.dynamic_slice_in_dim(whole, mine * share, share, 3)
    return (own_joined.astype(jnp.float32) + conv).astype(jnp.bfloat16)


def solution(mesh):
    return jax.shard_map(
        body,
        mesh=mesh,
        in_specs=(
            P(("clips", "tm"), "space", None, "chan"),
            P("clips", "space", None, None),
            P(),
            P(),
            P(),
            P(),
            P(),
            P(),
            P(None, None, None, None, "chan"),
        ),
        out_specs=P(("clips", "tm"), "space", None, "chan"),
        check_vma=False,
    )
```

profile of v0, /device:TPU:0, one launch (start us, length us, event | category | flops | bytes accessed | tf_op | source)
XLA Modules:
  0.0 116.3 jit_solution(1926624197613109839)
XLA Ops:
  6.6 5.2 %all_to_all.4 = bf16[1,4,160,192]{3,2,0,1:T(8,128)(2,1)S(1)} all-to-all(bf16[1,4,160,192]{3,2,0,1:T(8,128)(2,1)} %bitcast.55), channel_id=1, replica_groups=mesh['clips'=2,'space'=4,'tm'=2,'chan'=2] {'chan'}, dimensions={1} | all-to-all | bytes 491520 | tf_op jit(solution)/shard_map/all_to_all | solution.py:38
  11.8 0.3 copy.58
  12.1 0.5 reshape.60
  12.6 0.2 multiply_reduce_fusion
  13.0 0.8 multiply_convert_fusion
  13.8 1.3 %convolution_convert_fusion.2 = bf16[320,384]{1,0:T(8,128)(2,1)S(1)} fusion(bf16[320,384]{1,0:T(8,128)(2,1)} %multiply_convert_fusion, bf16[384,384]{1,0:T(8,128)(2,1)S(1)} %copy-done.2), kind=kOutput, calls=%fused_computation.32 | convolution fusion | flops 94494720 | bytes 786432 | tf_op jit(solution)/shard_map/dot_general | solution.py:42
  15.1 29.6 %all-gather.2.cloned.1.call-done = bf16[2560,384]{1,0:T(8,128)(2,1)} async-done(((bf16[320,384]{1,0:T(8,128)(2,1)}), bf16[2560,384]{1,0:T(8,128)(2,1)}) %all-gather.2.cloned.1.call-update) | async-done | bytes 1966096 | tf_op jit(solution)/shard_map/all_gather | solution.py:45
  44.7 5.4 %fusion.46 = (f32[320]{0:T(512)S(1)}, f32[320,2560]{1,0:T(8,128)}) fusion(bf16[320,384]{1,0:T(8,128)(2,1)S(1)} %convolution_convert_fusion.2, bf16[2560,384]{1,0:T(8,128)(2,1)} %all-gather.2.cloned.1.call-done, bf16[384,384]{1,0:T(8,128)(2,1)S(1)} %copy-done), kind=kOutput, calls=%fused_computation.64 | convolution fusion | flops 1386741504 | bytes 5784832 | tf_op jit(solution)/shard_map/qc,kc->qk/dot_general | solution.py:49
  50.1 2.6 %fusion.2 = f32[320]{0:T(512)S(1)} fusion(f32[320,2560]{1,0:T(8,128)} %get-tuple-element.10, f32[320]{0:T(512)S(1)} %broadcast_maximum_fusion), kind=kLoop, calls=%fused_computation.9 | loop fusion | flops 1638080 | bytes 3279360 | tf_op jit(solution)/shard_map/reduce_sum | solution.py:52
  52.7 4.8 %fusion.28 = bf16[320,384]{1,0:T(8,128)(2,1)S(1)} fusion(f32[320,2560]{1,0:T(8,128)} %get-tuple-element.10, f32[320]{0:T(512)S(1)} %broadcast_maximum_fusion, bf16[2560,384]{1,0:T(8,128)(2,1)} %all-gather.2.cloned.1.call-done, bf16[384,384]{1,0:T(8,128)(2,1)S(1)} %copy-done.7, f32[320]{0:T(512)S(1)} %fusion.2), kind=kOutput, calls=%fused_computation.35 | convolution fusion | flops 1386987520 | bytes 5786112 | tf_op jit(solution)/shard_map/dot_general | solution.py:53
  57.5 0.3 fusion.24
  57.9 2.2 %all_gather.7 = bf16[1,4,160,384]{3,2,0,1:T(8,128)(2,1)S(1)} all-gather(bf16[1,2,160,384]{3,2,0,1:T(8,128)(2,1)S(1)} %bitcast.53), channel_id=1, replica_groups=mesh['clips'=2,'space'=4,'tm'=2,'chan'=2] {'chan'}, dimensions={1}, use_global_device_ids=true | all-gather | bytes 737280 | tf_op jit(solution)/shard_map/all_gather | solution.py:60
  60.0 0.2 fusion.31
  60.3 0.4 fusion.38
  60.6 1.4 %collective-permute-start = (bf16[1,4,160,384]{3,2,0,1:T(8,128)(2,1)S(1)}, bf16[1,4,160,384]{3,2,0,1:T(8,128)(2,1)}, u32[]{:S(2)}, u32[]{:S(2)}) collective-permute-start(bf16[1,4,160,384]{3,2,0,1:T(8,128)(2,1)S(1)} %fusion.38), channel_id=1, source_target_pairs={} | collective-permute-start | bytes 1474568 | tf_op jit(solution)/shard_map/ppermute | solution.py:10
  62.1 4.2 %collective-permute-start.1 = (bf16[1,4,160,384]{3,2,0,1:T(8,128)(2,1)S(1)}, bf16[1,4,160,384]{3,2,0,1:T(8,128)(2,1)}, u32[]{:S(2)}, u32[]{:S(2)}) collective-permute-start(bf16[1,4,160,384]{3,2,0,1:T(8,128)(2,1)S(1)} %fusion.38), channel_id=1, source_target_pairs={{0,2},{1,3},{4,6},{5,7},{8,10},{9,11},{12,14},{13,15},{16,18},{17,... | collective-permute-start | bytes 1474568 | tf_op jit(solution)/shard_map/ppermute | solution.py:10
  66.2 10.1 %collective-permute-done.1 = bf16[1,4,160,384]{3,2,0,1:T(8,128)(2,1)} collective-permute-done((bf16[1,4,160,384]{3,2,0,1:T(8,128)(2,1)S(1)}, bf16[1,4,160,384]{3,2,0,1:T(8,128)(2,1)}, u32[]{:S(2)}, u32[]{:S(2)}) %collective-permute-start.1) | collective-permute-done | bytes 491552 | tf_op jit(solution)/shard_map/ppermute | solution.py:10
  76.3 1.1 fusion.41
  77.5 1.0 maximum_bitcast_fusion
  78.4 3.5 %collective-permute-start.2 = (bf16[3,1,160,384]{3,2,1,0:T(8,128)(2,1)}, bf16[3,1,160,384]{3,2,1,0:T(8,128)(2,1)S(1)}, u32[]{:S(2)}, u32[]{:S(2)}) collective-permute-start(bf16[3,1,160,384]{3,2,1,0:T(8,128)(2,1)} %get-tuple-element.5), channel_id=1, source_target_pairs={{0,4},{4,8},{8,12},{1,5},{5,9},{9,13},{2,6},{6,10},{10,14},{3,7},{... | collective-permute-start | bytes 1105928 | tf_op jit(solution)/shard_map/ppermute | solution.py:21
  81.9 1.5 %collective-permute-start.3 = (bf16[3,1,160,384]{3,2,1,0:T(8,128)(2,1)}, bf16[3,1,160,384]{3,2,1,0:T(8,128)(2,1)}, u32[]{:S(2)}, u32[]{:S(2)}) collective-permute-start(bf16[3,1,160,384]{3,2,1,0:T(8,128)(2,1)} %get-tuple-element.6), channel_id=1, source_target_pairs={{4,0},{8,4},{12,8},{5,1},{9,5},{13,9},{6,2},{10,6},{14,10},{7,3},{... | collective-permute-start | bytes 1105928 | tf_op jit(solution)/shard_map/ppermute | solution.py:23
  83.6 6.1 %collective-permute-done.2 = bf16[3,1,160,384]{3,2,1,0:T(8,128)(2,1)S(1)} collective-permute-done((bf16[3,1,160,384]{3,2,1,0:T(8,128)(2,1)}, bf16[3,1,160,384]{3,2,1,0:T(8,128)(2,1)S(1)}, u32[]{:S(2)}, u32[]{:S(2)}) %collective-permute-start.2) | collective-permute-done | bytes 368672 | tf_op jit(solution)/shard_map/ppermute | solution.py:21
  89.7 4.1 %collective-permute-done.3 = bf16[3,1,160,384]{3,2,1,0:T(8,128)(2,1)} collective-permute-done((bf16[3,1,160,384]{3,2,1,0:T(8,128)(2,1)}, bf16[3,1,160,384]{3,2,1,0:T(8,128)(2,1)}, u32[]{:S(2)}, u32[]{:S(2)}) %collective-permute-start.3) | collective-permute-done | bytes 368672 | tf_op jit(solution)/shard_map/ppermute | solution.py:23
  93.8 3.1 %fusion.11 = bf16[3,6,1,162,384]{4,3,0,1,2:T(8,128)(2,1)S(1)} fusion(bf16[3,1,160,384]{3,2,0,1:T(8,128)(2,1)} %bitcast.8, bf16[3,1,160,384]{3,2,0,1:T(8,128)(2,1)S(1)} %bitcast.54, bf16[1,4,160,384]{3,2,0,1:T(8,128)(2,1)S(1)} %fusion.38, bf16[1,4,160,384]{3,2,0,1:T(8,128)(2,1)S(1)} %get-tuple-element.8, bf16[1,4,160,384]{3,2,0,1:T(8,128)(2,1)S(1)} %get-tuple-element.7), kind=kLoop, calls=%fused_computation.18 | loop fusion | flops 20155392 | bytes 4451328 | tf_op jit(solution)/shard_map/broadcast_in_dim | solution.py:71
  96.9 1.6 %pad.5 = bf16[3,6,1,168,384]{4,3,0,1,2:T(8,128)(2,1)} pad(bf16[3,6,1,162,384]{4,3,0,1,2:T(8,128)(2,1)S(1)} %fusion.11, bf16[]{:T(256)} %constant.34.clone.1), padding=0_0x0_0x0_0x0_6x0_0 | pad | bytes 4561922 | tf_op jit(solution)/shard_map/broadcast_in_dim | solution.py:71
  98.5 3.5 %reshape.69 = bf16[3,6,1,8,21,384]{5,4,3,0,1,2:T(8,128)(2,1)S(1)} reshape(bf16[3,6,1,168,384]{4,3,0,1,2:T(8,128)(2,1)} %pad.5) | data formatting | bytes 4644864 | tf_op jit(solution)/shard_map/conv_general_dilated | solution.py:70
  102.1 0.3 copy.47
  102.4 1.7 %copy-done.6 = bf16[3,3,3,384,192]{3,4,2,1,0:T(8,128)(2,1)S(1)} copy-done((bf16[3,3,3,384,192]{3,4,2,1,0:T(8,128)(2,1)S(1)}, bf16[3,3,3,384,192]{3,4,2,1,0:T(8,128)(2,1)}, u32[]{:S(2)}) %copy-start.6) | copy-done | bytes 3981336
  104.2 3.9 %fusion.21 = f32[1,4,8,21,192]{4,2,3,1,0:T(8,128)S(1)} fusion(bf16[3,3,3,384,192]{3,4,2,1,0:T(8,128)(2,1)S(1)} %copy-done.6, bf16[3,6,1,7,2,384]{5,3,4,1,0,2:T(8,128)(2,1)S(1)} %slice.19, bf16[3,6,1,8,21,384]{5,3,4,1,0,2:T(8,128)(2,1)S(1)} %copy.47, pred[8,21]{0,1:T(8,128)(4,1)S(1)} %copy-done.8), kind=kOutput, calls=%fused_computation.28 | convolution fusion | flops 2683201536 | bytes 7013544 | tf_op jit(solution)/shard_map/conv_general_dilated | solution.py:70
  108.1 0.3 copy.48
  108.4 0.3 fusion.40
  108.7 0.8 copy.49
  (30 shorter events, 0.5 us)
Async XLA Ops:
  6.5 38.2 %copy-start = (bf16[384,384]{1,0:T(8,128)(2,1)S(1)}, bf16[384,384]{1,0:T(8,128)(2,1)}, u32[]{:S(2)}) copy-start(bf16[384,384]{1,0:T(8,128)(2,1)} %param.14) | copy-start | bytes 884740
  6.5 6.4 %copy-start.4 = (bf16[384]{0:T(512)(128)(2,1)S(1)}, bf16[384]{0:T(512)(128)(2,1)}, u32[]{:S(2)}) copy-start(bf16[384]{0:T(512)(128)(2,1)} %param.11) | copy-start | bytes 2308
  6.5 7.3 %copy-start.5 = (bf16[384]{0:T(512)(128)(2,1)S(1)}, bf16[384]{0:T(512)(128)(2,1)}, u32[]{:S(2)}) copy-start(bf16[384]{0:T(512)(128)(2,1)} %param.12) | copy-start | bytes 2308
  6.5 7.3 %copy-start.2 = (bf16[384,384]{1,0:T(8,128)(2,1)S(1)}, bf16[384,384]{1,0:T(8,128)(2,1)}, u32[]{:S(2)}) copy-start(bf16[384,384]{1,0:T(8,128)(2,1)} %param.13) | copy-start | bytes 884740
  6.5 38.1 %all-gather.2.cloned.1.call-start = ((), (), s32[]{:S(2)}) async-start(), calls=%async_computation.1 | async-start | bytes 2211840 | tf_op jit(solution)/shard_map/all_gather | solution.py:45
  50.1 2.6 %copy-start.7 = (bf16[384,384]{1,0:T(8,128)(2,1)S(1)}, bf16[384,384]{1,0:T(8,128)(2,1)}, u32[]{:S(2)}) copy-start(bf16[384,384]{1,0:T(8,128)(2,1)} %param.15) | copy-start | bytes 884740
  52.7 4.8 %copy-start.3 = (bf16[384,384]{1,0:T(8,128)(2,1)S(1)}, bf16[384,384]{1,0:T(8,128)(2,1)}, u32[]{:S(2)}) copy-start(bf16[384,384]{1,0:T(8,128)(2,1)} %param.16) | copy-start | bytes 884740
  57.5 18.8 %copy-start.1 = (bf16[2,4,160,384]{3,2,1,0:T(8,128)(2,1)S(1)}, bf16[2,4,160,384]{3,2,1,0:T(8,128)(2,1)}, u32[]{:S(2)}) copy-start(bf16[2,4,160,384]{3,2,1,0:T(8,128)(2,1)} %param.10) | copy-start | bytes 2949124
  60.6 5.6 %collective-permute-start = (bf16[1,4,160,384]{3,2,0,1:T(8,128)(2,1)S(1)}, bf16[1,4,160,384]{3,2,0,1:T(8,128)(2,1)}, u32[]{:S(2)}, u32[]{:S(2)}) collective-permute-start(bf16[1,4,160,384]{3,2,0,1:T(8,128)(2,1)S(1)} %fusion.38), channel_id=1, source_target_pairs={} | collective-permute-start | bytes 1474568 | tf_op jit(solution)/shard_map/ppermute | solution.py:10
  62.1 14.2 %collective-permute-start.1 = (bf16[1,4,160,384]{3,2,0,1:T(8,128)(2,1)S(1)}, bf16[1,4,160,384]{3,2,0,1:T(8,128)(2,1)}, u32[]{:S(2)}, u32[]{:S(2)}) collective-permute-start(bf16[1,4,160,384]{3,2,0,1:T(8,128)(2,1)S(1)} %fusion.38), channel_id=1, source_target_pairs={{0,2},{1,3},{4,6},{5,7},{8,10},{9,11},{12,14},{13,15},{16,18},{17,... | collective-permute-start | bytes 1474568 | tf_op jit(solution)/shard_map/ppermute | solution.py:10
  78.4 11.2 %collective-permute-start.2 = (bf16[3,1,160,384]{3,2,1,0:T(8,128)(2,1)}, bf16[3,1,160,384]{3,2,1,0:T(8,128)(2,1)S(1)}, u32[]{:S(2)}, u32[]{:S(2)}) collective-permute-start(bf16[3,1,160,384]{3,2,1,0:T(8,128)(2,1)} %get-tuple-element.5), channel_id=1, source_target_pairs={{0,4},{4,8},{8,12},{1,5},{5,9},{9,13},{2,6},{6,10},{10,14},{3,7},{... | collective-permute-start | bytes 1105928 | tf_op jit(solution)/shard_map/ppermute | solution.py:21
  81.9 11.9 %collective-permute-start.3 = (bf16[3,1,160,384]{3,2,1,0:T(8,128)(2,1)}, bf16[3,1,160,384]{3,2,1,0:T(8,128)(2,1)}, u32[]{:S(2)}, u32[]{:S(2)}) collective-permute-start(bf16[3,1,160,384]{3,2,1,0:T(8,128)(2,1)} %get-tuple-element.6), channel_id=1, source_target_pairs={{4,0},{8,4},{12,8},{5,1},{9,5},{13,9},{6,2},{10,6},{14,10},{7,3},{... | collective-permute-start | bytes 1105928 | tf_op jit(solution)/shard_map/ppermute | solution.py:23
  102.0 2.1 %copy-start.6 = (bf16[3,3,3,384,192]{3,4,2,1,0:T(8,128)(2,1)S(1)}, bf16[3,3,3,384,192]{3,4,2,1,0:T(8,128)(2,1)}, u32[]{:S(2)}) copy-start(bf16[3,3,3,384,192]{3,4,2,1,0:T(8,128)(2,1)} %param.17) | copy-start | bytes 11943940
  102.0 2.1 %copy-start.8 = (pred[8,21]{0,1:T(8,128)(4,1)S(1)}, pred[8,21]{0,1:T(8,128)(4,1)}, u32[]{:S(2)}) copy-start(pred[8,21]{0,1:T(8,128)(4,1)} %constant.42) | copy-start | bytes 508
Sparse Core Ops, SparseCore 0:
  13.9 30.7 all-gather.1
where the time goes:
time: 117 us; the launch traced here: 116 us
  waiting for transfers between devices  49.9 us (43%)
  matrix products  15.7 us (13%)
  between operations  13.6 us (12%)
  starting transfers between devices  10.6 us (9%)
  other arithmetic  9.76 us (8%)
  local copies, waits for them, and re-layouts  9.41 us (8%)
  blocking collectives  7.34 us (6%)
    all_gather x1, waiting for transfers between devices, body(): piece = lax.all_gather(normed, ('space', 'chan'), axis=0, tiled=True)  29.6 us
    ppermute x2, waiting for transfers between devices, from_behind(): return lax.ppermute(array, axis, pairs)  10.1 us
    ppermute x1, waiting for transfers between devices, padded_2(): lax.ppermute(tail, axis, [(i, (i + 1) % count) for i in range(ends)])  6.08 us
    ppermute x2, starting transfers between devices, from_behind(): return lax.ppermute(array, axis, pairs)  5.6 us
    dot_general x1, matrix products, body(): jnp.einsum('qc,kc->qk', query, keys, preferred_element_type=jnp.float32)  5.41 us
    all_to_all x1, blocking collectives, body(): lax.all_to_all(frames_in, 'chan', split_axis=1, concat_axis=3, tiled=True)  5.19 us
    dot_general x1, matrix products, body(): jnp.dot(weights.astype(jnp.bfloat16), values, preferred_element_type=jnp....  4.79 us
    ppermute x1, waiting for transfers between devices, padded_2(): lax.ppermute(head, axis, [((i + 1) % count, i) for i in range(ends)])  4.14 us
  transfers between devices with their start and end apart: 5, of which 4 were waited for; matrix products, arithmetic and copies ran while one was open for 1% of the time, Pallas kernels for 0%

commit v1 on v0

--- a/solution.py
+++ b/solution.py
@@ -2,6 +2,22 @@
 import jax.numpy as jnp
 from jax import lax
 from jax.sharding import PartitionSpec as P
+
+
+def gather_around(x, axis, dim):
+    ways, here, step = (lax.axis_size(axis), lax.axis_index(axis), x.shape[dim])
+    dims = [n * ways if d == dim else n for d, n in enumerate(x.shape)]
+    full = lax.dynamic_update_slice_in_dim(jnp.zeros(dims, x.dtype), x, here * step, axis=dim)
+    going_up = going_down = x
+    for far in range(1, ways // 2 + 1):
+        going_up = lax.ppermute(going_up, axis, [(d, (d + 1) % ways) for d in range(ways)])
+        full = lax.dynamic_update_slice_in_dim(full, going_up, (here - far) % ways * step, axis=dim)
+        if 2 * far < ways:
+            going_down = lax.ppermute(going_down, axis, [(d, (d - 1) % ways) for d in range(ways)])
+            full = lax.dynamic_update_slice_in_dim(
+                full, going_down, (here + far) % ways * step, axis=dim
+            )
+    return full
 
 
 def from_behind(array, axis, by):
@@ -42,7 +58,7 @@
     query = jnp.dot(normed, w_query, preferred_element_type=jnp.float32).astype(jnp.bfloat16)
     scale = width ** (-0.5)
     count = tokens.shape[0]
-    piece = lax.all_gather(normed, ("space", "chan"), axis=0, tiled=True)
+    piece = gather_around(normed, ("space", "chan"), 0)
     keys = jnp.dot(piece, w_key, preferred_element_type=jnp.float32).astype(jnp.bfloat16)
     values = jnp.dot(piece, w_value, preferred_element_type=jnp.float32).astype(jnp.bfloat16)
     top = jnp.full((count, 1), -1e30, jnp.float32)

time: 117 us -> 101 us (0.86)
  starting transfers between devices: 10.6 us -> 24.5 us
  between operations: 13.6 us -> 0.27 us
  waiting for transfers between devices: 49.9 us -> 37.3 us
  blocking collectives: 7.34 us -> 2.16 us
  local copies, waits for them, and re-layouts: 9.41 us -> 12.5 us
  other arithmetic: 9.76 us -> 7.99 us
    all_gather x1 -> x0, waiting for transfers between devices: 29.6 us -> none  [body(): piece = lax.all_gather(normed, ('space', 'chan'), axis=0, tiled=True)]
    ppermute x0 -> x7, waiting for transfers between devices: none -> 16.5 us  [the longest x4 13.2 us: gather_around(): lax.ppermute(going_up, axis, [(d, (d + 1) % ways) for d in range(ways)])]
    ppermute x0 -> x7, starting transfers between devices: none -> 12.2 us  [the longest x3 12 us: gather_around(): lax.ppermute(going_down, axis, [(d, (d - 1) % ways) for d in range(ways)])]
    all_to_all x1 -> x0, blocking collectives: 5.19 us -> none  [body(): lax.all_to_all(frames_in, 'chan', split_axis=1, concat_axis=3, tiled=True)]
    all_to_all x0 -> x1, starting transfers between devices: none -> 3.59 us  [body(): lax.all_to_all(frames_in, 'chan', split_axis=1, concat_axis=3, tiled=True)]
    dynamic_update_slice x0 -> x7, local copies, waits for them, and re-layouts: none -> 2.18 us  [the longest x4 1.11 us: gather_around(): lax.dynamic_update_slice_in_dim(full, going_up, (here - far) % ways * ste...]
    ppermute x1, starting transfers between devices: 3.47 us -> 1.3 us  [padded_2(): lax.ppermute(tail, axis, [(i, (i + 1) % count) for i in range(ends)])]
    all_to_all x0 -> x1, waiting for transfers between devices: none -> 1.58 us  [body(): lax.all_to_all(frames_in, 'chan', split_axis=1, concat_axis=3, tiled=True)]
  transfers between devices with their start and end apart: 5 -> 12, of which waited for: 4 -> 9; matrix products, arithmetic and copies ran while one was open for 1% -> 4% of each run, Pallas kernels for 0% -> 0%
where the time goes in v1:
time: 101 us
  waiting for transfers between devices  37.3 us (37%)
  starting transfers between devices  24.5 us (24%)
  matrix products  16 us (16%)
  local copies, waits for them, and re-layouts  12.5 us (12%)
  other arithmetic  7.99 us (8%)
  blocking collectives  2.16 us (2%)
    ppermute x4, waiting for transfers between devices, gather_around(): lax.ppermute(going_up, axis, [(d, (d + 1) % ways) for d in range(ways)])  13.2 us
    ppermute x3, starting transfers between devices, gather_around(): lax.ppermute(going_down, axis, [(d, (d - 1) % ways) for d in range(ways)])  12 us
    ppermute x2, waiting for transfers between devices, from_behind(): return lax.ppermute(array, axis, pairs)  9.99 us
    ppermute x2, starting transfers between devices, from_behind(): return lax.ppermute(array, axis, pairs)  5.96 us
    ppermute x1, waiting for transfers between devices, padded_2(): lax.ppermute(tail, axis, [(i, (i + 1) % count) for i in range(ends)])  5.5 us
    dot_general x1, matrix products, body(): jnp.dot(weights.astype(jnp.bfloat16), values, preferred_element_type=jnp....  4.88 us
    dot_general x1, matrix products, body(): jnp.einsum('qc,kc->qk', query, keys, preferred_element_type=jnp.float32)  4.85 us
    conv_general_dilated x4, local copies, waits for them, and re-layouts, body(): lax.conv_general_dilated(padded[None], conv_weight, (1, 1, 1), 'VALID', d...  4.14 us
  transfers between devices with their start and end apart: 12, of which 9 were waited for; matrix products, arithmetic and copies ran while one was open for 4% of the time, Pallas kernels for 0%

profile of v1, /device:TPU:0, one launch (start us, length us, event | category | flops | bytes accessed | tf_op | source)
XLA Modules:
  0.0 100.8 jit_solution(11818649885662151159)
XLA Ops:
  0.0 3.6 %all-to-all-start = ((bf16[1,4,160,192]{3,2,0,1:T(8,128)(2,1)}), bf16[1,4,160,192]{3,2,0,1:T(8,128)(2,1)S(1)}, u32[]{:S(2)}, u32[]{:S(2)}) async-start(bf16[1,4,160,192]{3,2,0,1:T(8,128)(2,1)} %bitcast.56), calls=%async_computation | async-start | bytes 655360 | tf_op jit(solution)/shard_map/all_to_all | solution.py:54
  3.6 1.6 %all-to-all-done = bf16[1,4,160,192]{3,2,0,1:T(8,128)(2,1)S(1)} async-done(((bf16[1,4,160,192]{3,2,0,1:T(8,128)(2,1)}), bf16[1,4,160,192]{3,2,0,1:T(8,128)(2,1)S(1)}, u32[]{:S(2)}, u32[]{:S(2)}) %all-to-all-start) | async-done | bytes 245792 | tf_op jit(solution)/shard_map/all_to_all | solution.py:54
  7.0 4.7 %collective-permute-start.1 = (bf16[320,384]{1,0:T(8,128)(2,1)S(1)}, bf16[320,384]{1,0:T(8,128)(2,1)}, u32[]{:S(2)}, u32[]{:S(2)}) collective-permute-start(bf16[320,384]{1,0:T(8,128)(2,1)S(1)} %get-tuple-element.6), channel_id=1, source_target_pairs={{0,13},{1,0},{4,1},{5,4},{8,5},{9,8},{12,9},{13,12},{2,15},{3,2},{... | collective-permute-start | bytes 737288 | tf_op jit(solution)/shard_map/ppermute | solution.py:16
  11.7 4.2 %collective-permute-done = bf16[320,384]{1,0:T(8,128)(2,1)} collective-permute-done((bf16[320,384]{1,0:T(8,128)(2,1)S(1)}, bf16[320,384]{1,0:T(8,128)(2,1)}, u32[]{:S(2)}, u32[]{:S(2)}) %collective-permute-start) | collective-permute-done | bytes 245792 | tf_op jit(solution)/shard_map/ppermute | solution.py:13
  15.9 3.7 %collective-permute-start.3 = (bf16[320,384]{1,0:T(8,128)(2,1)}, bf16[320,384]{1,0:T(8,128)(2,1)S(1)}, u32[]{:S(2)}, u32[]{:S(2)}) collective-permute-start(bf16[320,384]{1,0:T(8,128)(2,1)} %collective-permute-done.1), channel_id=1, source_target_pairs={{0,13},{1,0},{4,1},{5,4},{8,5},{9,8},{12,9},{13,12},{2,15},{3,2},{... | collective-permute-start | bytes 737288 | tf_op jit(solution)/shard_map/ppermute | solution.py:16
  19.6 1.0 %convolution_convert_fusion.2 = bf16[320,384]{1,0:T(8,128)(2,1)} fusion(bf16[320,384]{1,0:T(8,128)(2,1)S(1)} %get-tuple-element.6, bf16[384,384]{1,0:T(8,128)(2,1)S(1)} %copy-done.3), kind=kOutput, calls=%fused_computation.32 | convolution fusion | flops 94494720 | bytes 786432 | tf_op jit(solution)/shard_map/dot_general | solution.py:58
  20.6 3.0 %collective-permute-done.2 = bf16[320,384]{1,0:T(8,128)(2,1)S(1)} collective-permute-done((bf16[320,384]{1,0:T(8,128)(2,1)}, bf16[320,384]{1,0:T(8,128)(2,1)S(1)}, u32[]{:S(2)}, u32[]{:S(2)}) %collective-permute-start.2) | collective-permute-done | bytes 245792 | tf_op jit(solution)/shard_map/ppermute | solution.py:13
  23.7 1.0 constant_dynamic-update-slice_fusion.6
  24.6 1.0 constant_dynamic-update-slice_fusion.5
  25.6 3.6 %collective-permute-start.5 = (bf16[320,384]{1,0:T(8,128)(2,1)S(1)}, bf16[320,384]{1,0:T(8,128)(2,1)S(1)}, u32[]{:S(2)}, u32[]{:S(2)}) collective-permute-start(bf16[320,384]{1,0:T(8,128)(2,1)S(1)} %collective-permute-done.3), channel_id=1, source_target_pairs={{0,13},{1,0},{4,1},{5,4},{8,5},{9,8},{12,9},{13,12},{2,15},{3,2},{... | collective-permute-start | bytes 737288 | tf_op jit(solution)/shard_map/ppermute | solution.py:16
  29.3 1.9 %collective-permute-done.4 = bf16[320,384]{1,0:T(8,128)(2,1)S(1)} collective-permute-done((bf16[320,384]{1,0:T(8,128)(2,1)S(1)}, bf16[320,384]{1,0:T(8,128)(2,1)S(1)}, u32[]{:S(2)}, u32[]{:S(2)}) %collective-permute-start.4) | collective-permute-done | bytes 245792 | tf_op jit(solution)/shard_map/ppermute | solution.py:13
  31.3 3.2 %collective-permute-done.5 = bf16[320,384]{1,0:T(8,128)(2,1)S(1)} collective-permute-done((bf16[320,384]{1,0:T(8,128)(2,1)S(1)}, bf16[320,384]{1,0:T(8,128)(2,1)S(1)}, u32[]{:S(2)}, u32[]{:S(2)}) %collective-permute-start.5) | collective-permute-done | bytes 245792 | tf_op jit(solution)/shard_map/ppermute | solution.py:16
  34.5 4.1 %collective-permute-done.6 = bf16[320,384]{1,0:T(8,128)(2,1)S(1)} collective-permute-done((bf16[320,384]{1,0:T(8,128)(2,1)S(1)}, bf16[320,384]{1,0:T(8,128)(2,1)S(1)}, u32[]{:S(2)}, u32[]{:S(2)}) %collective-permute-start.6) | collective-permute-done | bytes 245792 | tf_op jit(solution)/shard_map/ppermute | solution.py:13
  38.7 4.9 %fusion.46 = (f32[320]{0:T(512)S(1)}, f32[320,2560]{1,0:T(8,128)}) fusion(bf16[320,384]{1,0:T(8,128)(2,1)} %convolution_convert_fusion.2, bf16[2560,384]{1,0:T(8,128)(2,1)S(1)} %constant_dynamic-update-slice_fusion, bf16[384,384]{1,0:T(8,128)(2,1)S(1)} %copy-done), kind=kOutput, calls=%fused_computation.72 | convolution fusion | flops 1386741504 | bytes 5784832 | tf_op jit(solution)/shard_map/qc,kc->qk/dot_general | solution.py:65
  43.6 2.6 %fusion.2 = f32[320]{0:T(512)S(1)} fusion(f32[320,2560]{1,0:T(8,128)} %get-tuple-element.12, f32[320]{0:T(512)S(1)} %broadcast_maximum_fusion), kind=kLoop, calls=%fused_computation.9 | loop fusion | flops 1638080 | bytes 3279360 | tf_op jit(solution)/shard_map/reduce_sum | solution.py:68
  46.1 4.9 %fusion.28 = bf16[320,384]{1,0:T(8,128)(2,1)} fusion(bf16[2560,384]{1,0:T(8,128)(2,1)S(1)} %constant_dynamic-update-slice_fusion, bf16[384,384]{1,0:T(8,128)(2,1)S(1)} %copy-done.8, f32[320,2560]{1,0:T(8,128)} %get-tuple-element.12, f32[320]{0:T(512)S(1)} %broadcast_maximum_fusion, f32[320]{0:T(512)S(1)} %fusion.2), kind=kOutput, calls=%fused_computation.35 | convolution fusion | flops 1386987520 | bytes 5786112 | tf_op jit(solution)/shard_map/dot_general | solution.py:69
  51.0 1.4 %fusion.24 = bf16[320,384]{1,0:T(8,128)(2,1)S(1)} fusion(f32[320,384]{1,0:T(8,128)S(1)} %reshape.60, bf16[320,384]{1,0:T(8,128)(2,1)} %fusion.28, bf16[384,384]{1,0:T(8,128)(2,1)S(1)} %copy-done.4), kind=kOutput, calls=%fused_computation.33 | convolution fusion | flops 94617600 | bytes 1277952 | tf_op jit(solution)/shard_map/dot_general | solution.py:72
  52.4 2.2 %all_gather.3 = bf16[1,4,160,384]{3,2,0,1:T(8,128)(2,1)S(1)} all-gather(bf16[1,2,160,384]{3,2,0,1:T(8,128)(2,1)S(1)} %bitcast.53), channel_id=1, replica_groups=mesh['clips'=2,'space'=4,'tm'=2,'chan'=2] {'chan'}, dimensions={1}, use_global_device_ids=true | all-gather | bytes 737280 | tf_op jit(solution)/shard_map/all_gather | solution.py:76
  55.2 1.4 %collective-permute-start.7 = (bf16[1,4,160,384]{3,2,0,1:T(8,128)(2,1)S(1)}, bf16[1,4,160,384]{3,2,0,1:T(8,128)(2,1)}, u32[]{:S(2)}, u32[]{:S(2)}) collective-permute-start(bf16[1,4,160,384]{3,2,0,1:T(8,128)(2,1)S(1)} %fusion.38), channel_id=1, source_target_pairs={} | collective-permute-start | bytes 1474568 | tf_op jit(solution)/shard_map/ppermute | solution.py:26
  56.6 4.5 %collective-permute-start.8 = (bf16[1,4,160,384]{3,2,0,1:T(8,128)(2,1)S(1)}, bf16[1,4,160,384]{3,2,0,1:T(8,128)(2,1)}, u32[]{:S(2)}, u32[]{:S(2)}) collective-permute-start(bf16[1,4,160,384]{3,2,0,1:T(8,128)(2,1)S(1)} %fusion.38), channel_id=1, source_target_pairs={{0,2},{1,3},{4,6},{5,7},{8,10},{9,11},{12,14},{13,15},{16,18},{17,... | collective-permute-start | bytes 1474568 | tf_op jit(solution)/shard_map/ppermute | solution.py:26
  61.1 10.0 %collective-permute-done.8 = bf16[1,4,160,384]{3,2,0,1:T(8,128)(2,1)} collective-permute-done((bf16[1,4,160,384]{3,2,0,1:T(8,128)(2,1)S(1)}, bf16[1,4,160,384]{3,2,0,1:T(8,128)(2,1)}, u32[]{:S(2)}, u32[]{:S(2)}) %collective-permute-start.8) | collective-permute-done | bytes 491552 | tf_op jit(solution)/shard_map/ppermute | solution.py:26
  71.1 1.1 %fusion.41 = (bf16[1,4,160,384]{3,2,0,1:T(8,128)(2,1)S(1)}, bf16[1,4,160,384]{3,2,0,1:T(8,128)(2,1)S(1)}) fusion(bf16[1,4,160,384]{3,2,0,1:T(8,128)(2,1)} %collective-permute-done.7, bf16[2,4,160,384]{3,2,1,0:T(8,128)(2,1)S(1)} %copy-done.2, pred[]{:T(512)S(6)} %eq.16, pred[]{:T(512)S(6)} %eq.15, bf16[1,4,160,384]{3,2,0,1:T(8,128)(2,1)} %collective-permute-done.8), kind=kLoop, calls=%fused_computation.51 | loop fusion | flops 737280 | bytes 2949122 | tf_op jit(solution)/shard_map/jit(_where)/select_n | solution.py:82
  73.1 1.3 %collective-permute-start.9 = (bf16[3,1,160,384]{3,2,1,0:T(8,128)(2,1)}, bf16[3,1,160,384]{3,2,1,0:T(8,128)(2,1)S(1)}, u32[]{:S(2)}, u32[]{:S(2)}) collective-permute-start(bf16[3,1,160,384]{3,2,1,0:T(8,128)(2,1)} %get-tuple-element.7), channel_id=1, source_target_pairs={{0,4},{4,8},{8,12},{1,5},{5,9},{9,13},{2,6},{6,10},{10,14},{3,7},{... | collective-permute-start | bytes 1105928 | tf_op jit(solution)/shard_map/ppermute | solution.py:37
  74.4 1.5 %collective-permute-start.10 = (bf16[3,1,160,384]{3,2,1,0:T(8,128)(2,1)S(1)}, bf16[3,1,160,384]{3,2,1,0:T(8,128)(2,1)S(1)}, u32[]{:S(2)}, u32[]{:S(2)}) collective-permute-start(bf16[3,1,160,384]{3,2,1,0:T(8,128)(2,1)S(1)} %get-tuple-element.8), channel_id=1, source_target_pairs={{4,0},{8,4},{12,8},{5,1},{9,5},{13,9},{6,2},{10,6},{14,10},{7,3},{... | collective-permute-start | bytes 1105928 | tf_op jit(solution)/shard_map/ppermute | solution.py:39
  75.9 0.9 constant_dynamic-slice_fusion
  76.8 5.5 %collective-permute-done.9 = bf16[3,1,160,384]{3,2,1,0:T(8,128)(2,1)S(1)} collective-permute-done((bf16[3,1,160,384]{3,2,1,0:T(8,128)(2,1)}, bf16[3,1,160,384]{3,2,1,0:T(8,128)(2,1)S(1)}, u32[]{:S(2)}, u32[]{:S(2)}) %collective-permute-start.9) | collective-permute-done | bytes 368672 | tf_op jit(solution)/shard_map/ppermute | solution.py:37
  82.3 3.8 %collective-permute-done.10 = bf16[3,1,160,384]{3,2,1,0:T(8,128)(2,1)S(1)} collective-permute-done((bf16[3,1,160,384]{3,2,1,0:T(8,128)(2,1)S(1)}, bf16[3,1,160,384]{3,2,1,0:T(8,128)(2,1)S(1)}, u32[]{:S(2)}, u32[]{:S(2)}) %collective-permute-start.10) | collective-permute-done | bytes 368672 | tf_op jit(solution)/shard_map/ppermute | solution.py:39
  86.1 2.1 %fusion.11 = bf16[3,6,1,162,384]{4,3,0,1,2:T(8,128)(2,1)S(1)} fusion(bf16[3,1,160,384]{3,2,0,1:T(8,128)(2,1)S(1)} %bitcast.55, bf16[3,1,160,384]{3,2,0,1:T(8,128)(2,1)S(1)} %bitcast.54, bf16[1,4,160,384]{3,2,0,1:T(8,128)(2,1)S(1)} %fusion.38, bf16[1,4,160,384]{3,2,0,1:T(8,128)(2,1)S(1)} %get-tuple-element.10, bf16[1,4,160,384]{3,2,0,1:T(8,128)(2,1)S(1)} %get-tuple-element.9), kind=kLoop, calls=%fused_computation.18 | loop fusion | flops 20155392 | bytes 4451328 | tf_op jit(solution)/shard_map/broadcast_in_dim | solution.py:87
  88.2 1.6 %pad.5 = bf16[3,6,1,168,384]{4,3,0,1,2:T(8,128)(2,1)} pad(bf16[3,6,1,162,384]{4,3,0,1,2:T(8,128)(2,1)S(1)} %fusion.11, bf16[]{:T(256)} %constant.72.clone.1), padding=0_0x0_0x0_0x0_6x0_0 | pad | bytes 4561922 | tf_op jit(solution)/shard_map/broadcast_in_dim | solution.py:87
  89.9 3.5 %reshape.69 = bf16[3,6,1,8,21,384]{5,4,3,0,1,2:T(8,128)(2,1)S(1)} reshape(bf16[3,6,1,168,384]{4,3,0,1,2:T(8,128)(2,1)} %pad.5) | data formatting | bytes 4644864 | tf_op jit(solution)/shard_map/conv_general_dilated | solution.py:86
  93.8 1.7 %copy-done.7 = bf16[3,3,3,384,192]{3,4,2,1,0:T(8,128)(2,1)S(1)} copy-done((bf16[3,3,3,384,192]{3,4,2,1,0:T(8,128)(2,1)S(1)}, bf16[3,3,3,384,192]{3,4,2,1,0:T(8,128)(2,1)}, u32[]{:S(2)}) %copy-start.7) | copy-done | bytes 3981336
  95.5 3.9 %fusion.21 = f32[1,4,8,21,192]{4,2,3,1,0:T(8,128)S(1)} fusion(bf16[3,3,3,384,192]{3,4,2,1,0:T(8,128)(2,1)S(1)} %copy-done.7, bf16[3,6,1,7,2,384]{5,3,4,1,0,2:T(8,128)(2,1)S(1)} %slice.19, bf16[3,6,1,8,21,384]{5,3,4,1,0,2:T(8,128)(2,1)S(1)} %copy.47, pred[8,21]{0,1:T(8,128)(4,1)S(1)} %copy-done.9), kind=kOutput, calls=%fused_computation.28 | convolution fusion | flops 2683201536 | bytes 7013544 | tf_op jit(solution)/shard_map/conv_general_dilated | solution.py:86
  (52 shorter events, 5.1 us)
Async XLA Ops:
  0.0 38.7 %copy-start = (bf16[384,384]{1,0:T(8,128)(2,1)S(1)}, bf16[384,384]{1,0:T(8,128)(2,1)}, u32[]{:S(2)}) copy-start(bf16[384,384]{1,0:T(8,128)(2,1)} %param.14) | copy-start | bytes 884740
  0.0 6.4 %copy-start.5 = (bf16[384]{0:T(512)(128)(2,1)S(1)}, bf16[384]{0:T(512)(128)(2,1)}, u32[]{:S(2)}) copy-start(bf16[384]{0:T(512)(128)(2,1)} %param.11) | copy-start | bytes 2308
  0.0 5.2 %all-to-all-start = ((bf16[1,4,160,192]{3,2,0,1:T(8,128)(2,1)}), bf16[1,4,160,192]{3,2,0,1:T(8,128)(2,1)S(1)}, u32[]{:S(2)}, u32[]{:S(2)}) async-start(bf16[1,4,160,192]{3,2,0,1:T(8,128)(2,1)} %bitcast.56), calls=%async_computation | async-start | bytes 655360 | tf_op jit(solution)/shard_map/all_to_all | solution.py:54
  5.5 14.1 %copy-start.3 = (bf16[384,384]{1,0:T(8,128)(2,1)S(1)}, bf16[384,384]{1,0:T(8,128)(2,1)}, u32[]{:S(2)}) copy-start(bf16[384,384]{1,0:T(8,128)(2,1)} %param.13) | copy-start | bytes 884740
  6.0 14.6 %copy-start.6 = (bf16[384]{0:T(512)(128)(2,1)S(1)}, bf16[384]{0:T(512)(128)(2,1)}, u32[]{:S(2)}) copy-start(bf16[384]{0:T(512)(128)(2,1)} %param.12) | copy-start | bytes 2308
  6.8 9.1 %collective-permute-start = (bf16[320,384]{1,0:T(8,128)(2,1)S(1)}, bf16[320,384]{1,0:T(8,128)(2,1)}, u32[]{:S(2)}, u32[]{:S(2)}) collective-permute-start(bf16[320,384]{1,0:T(8,128)(2,1)S(1)} %get-tuple-element.6), channel_id=1, source_target_pairs={{0,1},{1,4},{4,5},{5,8},{8,9},{9,12},{12,13},{13,0},{2,3},{3,6},{6... | collective-permute-start | bytes 737288 | tf_op jit(solution)/shard_map/ppermute | solution.py:13
  7.0 8.9 %collective-permute-start.1 = (bf16[320,384]{1,0:T(8,128)(2,1)S(1)}, bf16[320,384]{1,0:T(8,128)(2,1)}, u32[]{:S(2)}, u32[]{:S(2)}) collective-permute-start(bf16[320,384]{1,0:T(8,128)(2,1)S(1)} %get-tuple-element.6), channel_id=1, source_target_pairs={{0,13},{1,0},{4,1},{5,4},{8,5},{9,8},{12,9},{13,12},{2,15},{3,2},{... | collective-permute-start | bytes 737288 | tf_op jit(solution)/shard_map/ppermute | solution.py:16
  15.9 7.8 %collective-permute-start.2 = (bf16[320,384]{1,0:T(8,128)(2,1)}, bf16[320,384]{1,0:T(8,128)(2,1)S(1)}, u32[]{:S(2)}, u32[]{:S(2)}) collective-permute-start(bf16[320,384]{1,0:T(8,128)(2,1)} %collective-permute-done), channel_id=1, source_target_pairs={{0,1},{1,4},{4,5},{5,8},{8,9},{9,12},{12,13},{13,0},{2,3},{3,6},{6... | collective-permute-start | bytes 737288 | tf_op jit(solution)/shard_map/ppermute | solution.py:13
  15.9 9.8 %collective-permute-start.3 = (bf16[320,384]{1,0:T(8,128)(2,1)}, bf16[320,384]{1,0:T(8,128)(2,1)S(1)}, u32[]{:S(2)}, u32[]{:S(2)}) collective-permute-start(bf16[320,384]{1,0:T(8,128)(2,1)} %collective-permute-done.1), channel_id=1, source_target_pairs={{0,13},{1,0},{4,1},{5,4},{8,5},{9,8},{12,9},{13,12},{2,15},{3,2},{... | collective-permute-start | bytes 737288 | tf_op jit(solution)/shard_map/ppermute | solution.py:16
  23.6 7.5 %collective-permute-start.4 = (bf16[320,384]{1,0:T(8,128)(2,1)S(1)}, bf16[320,384]{1,0:T(8,128)(2,1)S(1)}, u32[]{:S(2)}, u32[]{:S(2)}) collective-permute-start(bf16[320,384]{1,0:T(8,128)(2,1)S(1)} %collective-permute-done.2), channel_id=1, source_target_pairs={{0,1},{1,4},{4,5},{5,8},{8,9},{9,12},{12,13},{13,0},{2,3},{3,6},{6... | collective-permute-start | bytes 737288 | tf_op jit(solution)/shard_map/ppermute | solution.py:13
  25.6 8.8 %collective-permute-start.5 = (bf16[320,384]{1,0:T(8,128)(2,1)S(1)}, bf16[320,384]{1,0:T(8,128)(2,1)S(1)}, u32[]{:S(2)}, u32[]{:S(2)}) collective-permute-start(bf16[320,384]{1,0:T(8,128)(2,1)S(1)} %collective-permute-done.3), channel_id=1, source_target_pairs={{0,13},{1,0},{4,1},{5,4},{8,5},{9,8},{12,9},{13,12},{2,15},{3,2},{... | collective-permute-start | bytes 737288 | tf_op jit(solution)/shard_map/ppermute | solution.py:16
  31.2 7.5 %collective-permute-start.6 = (bf16[320,384]{1,0:T(8,128)(2,1)S(1)}, bf16[320,384]{1,0:T(8,128)(2,1)S(1)}, u32[]{:S(2)}, u32[]{:S(2)}) collective-permute-start(bf16[320,384]{1,0:T(8,128)(2,1)S(1)} %collective-permute-done.4), channel_id=1, source_target_pairs={{0,1},{1,4},{4,5},{5,8},{8,9},{9,12},{12,13},{13,0},{2,3},{3,6},{6... | collective-permute-start | bytes 737288 | tf_op jit(solution)/shard_map/ppermute | solution.py:13
  43.6 2.6 %copy-start.8 = (bf16[384,384]{1,0:T(8,128)(2,1)S(1)}, bf16[384,384]{1,0:T(8,128)(2,1)}, u32[]{:S(2)}) copy-start(bf16[384,384]{1,0:T(8,128)(2,1)} %param.15) | copy-start | bytes 884740
  46.1 4.9 %copy-start.4 = (bf16[384,384]{1,0:T(8,128)(2,1)S(1)}, bf16[384,384]{1,0:T(8,128)(2,1)}, u32[]{:S(2)}) copy-start(bf16[384,384]{1,0:T(8,128)(2,1)} %param.16) | copy-start | bytes 884740
  51.0 20.1 %copy-start.2 = (bf16[2,4,160,384]{3,2,1,0:T(8,128)(2,1)S(1)}, bf16[2,4,160,384]{3,2,1,0:T(8,128)(2,1)}, u32[]{:S(2)}) copy-start(bf16[2,4,160,384]{3,2,1,0:T(8,128)(2,1)} %param.10) | copy-start | bytes 2949124
  55.2 6.0 %collective-permute-start.7 = (bf16[1,4,160,384]{3,2,0,1:T(8,128)(2,1)S(1)}, bf16[1,4,160,384]{3,2,0,1:T(8,128)(2,1)}, u32[]{:S(2)}, u32[]{:S(2)}) collective-permute-start(bf16[1,4,160,384]{3,2,0,1:T(8,128)(2,1)S(1)} %fusion.38), channel_id=1, source_target_pairs={} | collective-permute-start | bytes 1474568 | tf_op jit(solution)/shard_map/ppermute | solution.py:26
  56.6 14.5 %collective-permute-start.8 = (bf16[1,4,160,384]{3,2,0,1:T(8,128)(2,1)S(1)}, bf16[1,4,160,384]{3,2,0,1:T(8,128)(2,1)}, u32[]{:S(2)}, u32[]{:S(2)}) collective-permute-start(bf16[1,4,160,384]{3,2,0,1:T(8,128)(2,1)S(1)} %fusion.38), channel_id=1, source_target_pairs={{0,2},{1,3},{4,6},{5,7},{8,10},{9,11},{12,14},{13,15},{16,18},{17,... | collective-permute-start | bytes 1474568 | tf_op jit(solution)/shard_map/ppermute | solution.py:26
  73.1 9.2 %collective-permute-start.9 = (bf16[3,1,160,384]{3,2,1,0:T(8,128)(2,1)}, bf16[3,1,160,384]{3,2,1,0:T(8,128)(2,1)S(1)}, u32[]{:S(2)}, u32[]{:S(2)}) collective-permute-start(bf16[3,1,160,384]{3,2,1,0:T(8,128)(2,1)} %get-tuple-element.7), channel_id=1, source_target_pairs={{0,4},{4,8},{8,12},{1,5},{5,9},{9,13},{2,6},{6,10},{10,14},{3,7},{... | collective-permute-start | bytes 1105928 | tf_op jit(solution)/shard_map/ppermute | solution.py:37
  74.4 11.7 %collective-permute-start.10 = (bf16[3,1,160,384]{3,2,1,0:T(8,128)(2,1)S(1)}, bf16[3,1,160,384]{3,2,1,0:T(8,128)(2,1)S(1)}, u32[]{:S(2)}, u32[]{:S(2)}) collective-permute-start(bf16[3,1,160,384]{3,2,1,0:T(8,128)(2,1)S(1)} %get-tuple-element.8), channel_id=1, source_target_pairs={{4,0},{8,4},{12,8},{5,1},{9,5},{13,9},{6,2},{10,6},{14,10},{7,3},{... | collective-permute-start | bytes 1105928 | tf_op jit(solution)/shard_map/ppermute | solution.py:39
  93.4 2.1 %copy-start.7 = (bf16[3,3,3,384,192]{3,4,2,1,0:T(8,128)(2,1)S(1)}, bf16[3,3,3,384,192]{3,4,2,1,0:T(8,128)(2,1)}, u32[]{:S(2)}) copy-start(bf16[3,3,3,384,192]{3,4,2,1,0:T(8,128)(2,1)} %param.17) | copy-start | bytes 11943940
  93.4 2.1 %copy-start.9 = (pred[8,21]{0,1:T(8,128)(4,1)S(1)}, pred[8,21]{0,1:T(8,128)(4,1)}, u32[]{:S(2)}) copy-start(pred[8,21]{0,1:T(8,128)(4,1)} %constant.101) | copy-start | bytes 508
  95.5 4.2 %copy-start.1 = (bf16[1,4,160,192]{3,2,0,1:T(8,128)(2,1)S(1)}, bf16[1,4,160,192]{3,2,0,1:T(8,128)(2,1)}, u32[]{:S(2)}) copy-start(bf16[1,4,160,192]{3,2,0,1:T(8,128)(2,1)} %constant_dynamic-slice_fusion) | copy-start | bytes 737284
